TPU v7x, 32 devices: a whole 2x2x4 slice. The times are simulated.
32 devices in a mesh: groups: 2 (over y), rows: 4 (over z), cols: 4 (over x, core).
Axes of the slice: x: 2, y: 2, z: 4, core: 2. Of those that a mesh axis runs over, the one named last changes fastest.
Arguments:
- coupling: bfloat16 [6, 8192, 8192], P('groups', 'cols', 'rows'), parts along dimension 0, may hold values from -0.0625 to 0.0625
- diag_inverse: bfloat16 [6, 8192, 8192], P('groups', 'rows', 'cols'), parts along dimension 0, as said below
- loads: bfloat16 [6, 128, 8192], P('groups', None, 'cols'), parts along dimension 0, may hold values from -6 to 6
- axle_index: int32 [64], P('groups'), parts along dimension 0, may hold values from 0 to 127
Outputs:
- influence: float32 [6, 32, 8192], P('groups', None, 'cols'), parts along dimension 0
- forward: float32 [6, 32, 8192], P('groups', None, 'rows'), parts along dimension 0
There are 2 independent parts, one for each index of `groups`. A program takes and returns all parts, laid end to end along the dimension named above; each array names one. Nothing has to cross between parts.
Inputs may be any that keep to these rules, and one draw needn't show every extreme that they name: `diag_inverse`: lower triangular with a positive diagonal.
All inputs are finite; a program needn't handle non-finite values.
Results may differ from a plain program's by a relative error of at most 0.0065.
Values sent between devices are 32-bit elements; how exact they have to be, the bound alone decides.
No kernel may reach another device: no remote copies, remote signals or barrier semaphores. Data moves between devices by JAX's collectives and lax.ppermute only.
A program may use at most 128 MiB of HBM per device.

v0:
```python
import jax
import jax.numpy as jnp
from jax import lax
from jax.sharding import PartitionSpec as P

LEVELS = 3


def pair_index(high, low):
    return high * (high - 1) // 2 + low


def forward_couple(partial_value):
    return lax.psum(partial_value, "rows")


def forward_diag(resid, tile):
    partial_value = jnp.einsum(
        "lm,im->li", resid.astype(jnp.bfloat16), tile, preferred_element_type=jnp.float32
    )
    return lax.psum(partial_value, "cols")


def backward_couple(partial_value):
    return lax.psum(partial_value, "cols")


def backward_diag(resid, tile):
    partial_value = jnp.einsum(
        "li,im->lm", resid.astype(jnp.bfloat16), tile, preferred_element_type=jnp.float32
    )
    return lax.psum(partial_value, "rows")


def lower_term(vector_bf, block):
    return jnp.einsum("lj,ij->li", vector_bf, block, preferred_element_type=jnp.float32)


def upper_term(vector_bf, block):
    return jnp.einsum("li,ij->lj", vector_bf, block, preferred_element_type=jnp.float32)


def solve_batch(rhs, coupling, diag_inverse):
    solved = []
    solved_bf = []
    for level in range(LEVELS):
        resid = rhs[level]
        if level > 0:
            partial_value = lower_term(solved_bf[0], coupling[pair_index(level, 0)])
            for lower in range(1, level):
                partial_value = partial_value + lower_term(
                    solved_bf[lower], coupling[pair_index(level, lower)]
                )
            resid = resid - forward_couple(partial_value)
        value = forward_diag(resid, diag_inverse[level])
        solved.append(value)
        solved_bf.append(value.astype(jnp.bfloat16))
    answers = [None] * LEVELS
    answers_bf = [None] * LEVELS
    for level in range(LEVELS - 1, -1, -1):
        resid = solved[level]
        if level < LEVELS - 1:
            partial_value = upper_term(
                answers_bf[LEVELS - 1], coupling[pair_index(LEVELS - 1, level)]
            )
            for upper in range(level + 1, LEVELS - 1):
                partial_value = partial_value + upper_term(
                    answers_bf[upper], coupling[pair_index(upper, level)]
                )
            resid = resid - backward_couple(partial_value)
        value = backward_diag(resid, diag_inverse[level])
        answers[level] = value
        answers_bf[level] = value.astype(jnp.bfloat16)
    return (jnp.stack(answers), jnp.stack(solved))


def body(coupling, diag_inverse, loads, axle_index):
    positions = loads.shape[1]
    selector = (axle_index[:, None] == jnp.arange(positions, dtype=jnp.int32)[None, :]).astype(
        jnp.bfloat16
    )
    rhs = jnp.einsum("lp,kpc->klc", selector, loads, preferred_element_type=jnp.float32)
    answer, solved = solve_batch(rhs, coupling, diag_inverse)
    return (answer, solved)


def solution(mesh):
    placed = (
        P("groups", "cols", "rows"),
        P("groups", "rows", "cols"),
        P("groups", None, "cols"),
        P("groups"),
    )
    return jax.shard_map(
        body,
        mesh=mesh,
        in_specs=placed,
        out_specs=(P("groups", None, "cols"), P("groups", None, "rows")),
        check_vma=False,
    )
```

profile of v0, /device:TPU:0, one launch (start us, length us, event | category | flops | bytes accessed | tf_op | source)
XLA Modules:
  0.0 431.7 jit_solution(7310455258160250758)
XLA Ops:
  7.2 0.0 copy-start
  7.2 0.0 all-reduce.11.cloned.1.call-start
  7.2 1.4 copy-done
  8.6 1.0 convolution_bitcast_fusion
  9.6 6.7 %fusion.22 = f32[32,2048]{1,0:T(8,128)} fusion(bf16[3,2048,2048]{2,1,0:T(8,128)(2,1)} %param.5, f32[3,32,2048]{2,1,0:T(8,128)S(1)} %convolution_bitcast_fusion), kind=kOutput, calls=%fused_computation.22 | convolution fusion | flops 268435456 | bytes 8781824 | tf_op jit(solution)/shard_map/lm,im->li/dot_general | solution.py:18
  16.3 0.0 all-reduce.11.cloned.1.call-update
  16.3 0.0 all-reduce.13.cloned.1.call-start
  16.4 34.8 %all-reduce.11.cloned.1.call-done = f32[32,2048]{1,0:T(8,128)} async-done(((f32[32,2048]{1,0:T(8,128)}), f32[32,2048]{1,0:T(8,128)}) %all-reduce.11.cloned.1.call-update) | async-done | bytes 262160 | tf_op jit(solution)/shard_map/psum | solution.py:21
  51.1 6.8 %fusion.14 = f32[32,2048]{1,0:T(8,128)} fusion(bf16[3,2048,2048]{2,1,0:T(8,128)(2,1)} %param.4, f32[32,2048]{1,0:T(8,128)} %all-reduce.11.cloned.1.call-done), kind=kOutput, calls=%fused_computation.14 | convolution fusion | flops 268500992 | bytes 8912896 | tf_op jit(solution)/shard_map/lj,ij->li/dot_general | solution.py:36
  57.9 0.0 all-reduce.13.cloned.1.call-update
  58.0 0.0 all-reduce.15.cloned.1.call-start
  58.0 35.4 %all-reduce.13.cloned.1.call-done = f32[32,2048]{1,0:T(8,128)} async-done(((f32[32,2048]{1,0:T(8,128)}), f32[32,2048]{1,0:T(8,128)}) %all-reduce.13.cloned.1.call-update) | async-done | bytes 262160 | tf_op jit(solution)/shard_map/psum | solution.py:14
  93.4 6.8 %fusion.10 = f32[32,2048]{1,0:T(8,128)} fusion(bf16[3,2048,2048]{2,1,0:T(8,128)(2,1)} %param.5, f32[32,2048]{1,0:T(8,128)} %all-reduce.13.cloned.1.call-done, f32[3,32,2048]{2,1,0:T(8,128)S(1)} %convolution_bitcast_fusion), kind=kOutput, calls=%fused_computation.10 | convolution fusion | flops 268566528 | bytes 9175040 | tf_op jit(solution)/shard_map/lm,im->li/dot_general | solution.py:18
  100.2 0.0 all-reduce.15.cloned.1.call-update
  100.2 0.0 all-reduce.17.cloned.1.call-start
  100.3 31.8 %all-reduce.15.cloned.1.call-done = f32[32,2048]{1,0:T(8,128)} async-done(((f32[32,2048]{1,0:T(8,128)}), f32[32,2048]{1,0:T(8,128)}) %all-reduce.15.cloned.1.call-update) | async-done | bytes 262160 | tf_op jit(solution)/shard_map/psum | solution.py:21
  132.1 6.1 %fusion.6 = f32[32,2048]{1,0:T(8,128)S(1)} fusion(bf16[3,2048,2048]{2,1,0:T(8,128)(2,1)} %param.4, f32[32,2048]{1,0:T(8,128)} %all-reduce.15.cloned.1.call-done), kind=kOutput, calls=%fused_computation.6 | convolution fusion | flops 268500992 | bytes 8912896 | tf_op jit(solution)/shard_map/lj,ij->li/dot_general | solution.py:36
  138.2 0.0 copy-done.1
  138.2 6.7 %fusion.39 = f32[32,2048]{1,0:T(8,128)} fusion(f32[32,2048]{1,0:T(8,128)S(1)} %fusion.6, bf16[3,2048,2048]{2,1,0:T(8,128)(2,1)} %param.4, f32[32,2048]{1,0:T(8,128)S(1)} %copy-done.1), kind=kOutput, calls=%fused_computation.38 | convolution fusion | flops 268566528 | bytes 9175040 | tf_op jit(solution)/shard_map/lj,ij->li/dot_general | solution.py:36
  144.9 0.0 all-reduce.17.cloned.1.call-update
  144.9 0.2 all-reduce.19.cloned.1.call-start
  145.1 35.3 %all-reduce.17.cloned.1.call-done = f32[32,2048]{1,0:T(8,128)} async-done(((f32[32,2048]{1,0:T(8,128)}), f32[32,2048]{1,0:T(8,128)}) %all-reduce.17.cloned.1.call-update) | async-done | bytes 262160 | tf_op jit(solution)/shard_map/psum | solution.py:14
  180.4 6.8 %fusion.2 = f32[32,2048]{1,0:T(8,128)} fusion(bf16[3,2048,2048]{2,1,0:T(8,128)(2,1)} %param.5, f32[32,2048]{1,0:T(8,128)} %all-reduce.17.cloned.1.call-done, f32[3,32,2048]{2,1,0:T(8,128)S(1)} %convolution_bitcast_fusion), kind=kOutput, calls=%fused_computation.2 | convolution fusion | flops 268566528 | bytes 9175040 | tf_op jit(solution)/shard_map/lm,im->li/dot_general | solution.py:18
  187.2 0.0 all-reduce.19.cloned.1.call-update
  187.2 0.0 all-reduce.21.cloned.1.call-start
  187.2 31.8 %all-reduce.19.cloned.1.call-done = f32[32,2048]{1,0:T(8,128)} async-done(((f32[32,2048]{1,0:T(8,128)}), f32[32,2048]{1,0:T(8,128)}) %all-reduce.19.cloned.1.call-update) | async-done | bytes 262160 | tf_op jit(solution)/shard_map/psum | solution.py:21
  219.0 5.7 %fusion = f32[32,2048]{1,0:T(8,128)} fusion(bf16[3,2048,2048]{2,1,0:T(8,128)(2,1)} %param.5, f32[32,2048]{1,0:T(8,128)} %all-reduce.19.cloned.1.call-done), kind=kOutput, calls=%fused_computation | convolution fusion | flops 268500992 | bytes 8912896 | tf_op jit(solution)/shard_map/li,im->lm/dot_general | solution.py:29
  224.8 0.0 all-reduce.21.cloned.1.call-update
  224.8 0.0 all-reduce.23.cloned.1.call-start
  224.8 35.4 %all-reduce.21.cloned.1.call-done = f32[32,2048]{1,0:T(8,128)} async-done(((f32[32,2048]{1,0:T(8,128)}), f32[32,2048]{1,0:T(8,128)}) %all-reduce.21.cloned.1.call-update) | async-done | bytes 262160 | tf_op jit(solution)/shard_map/psum | solution.py:32
  260.3 5.7 %fusion.4 = f32[32,2048]{1,0:T(8,128)} fusion(bf16[3,2048,2048]{2,1,0:T(8,128)(2,1)} %param.4, f32[32,2048]{1,0:T(8,128)} %all-reduce.21.cloned.1.call-done), kind=kOutput, calls=%fused_computation.4 | convolution fusion | flops 268500992 | bytes 8912896 | tf_op jit(solution)/shard_map/li,ij->lj/dot_general | solution.py:40
  266.0 0.0 all-reduce.23.cloned.1.call-update
  266.0 0.0 all-reduce.25.cloned.1.call-start
  266.1 31.8 %all-reduce.23.cloned.1.call-done = f32[32,2048]{1,0:T(8,128)} async-done(((f32[32,2048]{1,0:T(8,128)}), f32[32,2048]{1,0:T(8,128)}) %all-reduce.23.cloned.1.call-update) | async-done | bytes 262160 | tf_op jit(solution)/shard_map/psum | solution.py:25
  297.9 5.7 %fusion.8 = f32[32,2048]{1,0:T(8,128)} fusion(bf16[3,2048,2048]{2,1,0:T(8,128)(2,1)} %param.5, f32[32,2048]{1,0:T(8,128)S(1)} %copy-done.2, f32[32,2048]{1,0:T(8,128)} %all-reduce.23.cloned.1.call-done), kind=kOutput, calls=%fused_computation.8 | convolution fusion | flops 268566528 | bytes 9175040 | tf_op jit(solution)/shard_map/li,im->lm/dot_general | solution.py:29
  303.6 0.0 all-reduce.25.cloned.1.call-update
  303.6 0.0 all-reduce.27.cloned.1.call-start
  303.7 35.4 %all-reduce.25.cloned.1.call-done = f32[32,2048]{1,0:T(8,128)} async-done(((f32[32,2048]{1,0:T(8,128)}), f32[32,2048]{1,0:T(8,128)}) %all-reduce.25.cloned.1.call-update) | async-done | bytes 262160 | tf_op jit(solution)/shard_map/psum | solution.py:32
  339.1 5.0 %fusion.12 = f32[32,2048]{1,0:T(8,128)S(1)} fusion(bf16[3,2048,2048]{2,1,0:T(8,128)(2,1)} %param.4, f32[32,2048]{1,0:T(8,128)} %all-reduce.25.cloned.1.call-done), kind=kOutput, calls=%fused_computation.12 | convolution fusion | flops 268500992 | bytes 8912896 | tf_op jit(solution)/shard_map/li,ij->lj/dot_general | solution.py:40
  344.2 5.7 %fusion.42 = f32[32,2048]{1,0:T(8,128)} fusion(f32[32,2048]{1,0:T(8,128)S(1)} %fusion.12, bf16[3,2048,2048]{2,1,0:T(8,128)(2,1)} %param.4, f32[32,2048]{1,0:T(8,128)S(1)} %copy-done.3), kind=kOutput, calls=%fused_computation.39 | convolution fusion | flops 268566528 | bytes 9175040 | tf_op jit(solution)/shard_map/li,ij->lj/dot_general | solution.py:40
  349.9 0.0 all-reduce.27.cloned.1.call-update
  349.9 0.0 all-reduce.29.cloned.1.call-start
  349.9 31.8 %all-reduce.27.cloned.1.call-done = f32[32,2048]{1,0:T(8,128)} async-done(((f32[32,2048]{1,0:T(8,128)}), f32[32,2048]{1,0:T(8,128)}) %all-reduce.27.cloned.1.call-update) | async-done | bytes 262160 | tf_op jit(solution)/shard_map/psum | solution.py:25
  381.7 5.7 %fusion.36 = f32[1,32,2048]{2,1,0:T(8,128)} fusion(bf16[3,2048,2048]{2,1,0:T(8,128)(2,1)} %param.5, f32[32,2048]{1,0:T(8,128)S(1)} %copy-done.1, f32[32,2048]{1,0:T(8,128)} %all-reduce.27.cloned.1.call-done), kind=kOutput, calls=%fused_computation.37 | convolution fusion | flops 268566528 | bytes 9175040 | tf_op jit(solution)/shard_map/li,im->lm/dot_general | solution.py:29
  387.5 0.0 all-reduce.29.cloned.1.call-update
  387.5 0.9 pad_maximum_fusion.1
  388.4 34.5 %all-reduce.29.cloned.1.call-done = f32[1,32,2048]{2,1,0:T(8,128)} async-done(((f32[1,32,2048]{2,1,0:T(8,128)}), f32[1,32,2048]{2,1,0:T(8,128)}) %all-reduce.29.cloned.1.call-update) | async-done | bytes 262160 | tf_op jit(solution)/shard_map/psum | solution.py:32
  423.0 1.9 pad_maximum_fusion
  (9 shorter events, 0.0 us)
Async XLA Ops:
  7.2 1.4 copy-start
  7.2 44.0 %all-reduce.11.cloned.1.call-start = ((), (), s32[]{:S(2)}) async-start(), calls=%async_computation | async-start | bytes 524288 | tf_op jit(solution)/shard_map/psum | solution.py:21
  16.3 77.1 %all-reduce.13.cloned.1.call-start = ((), (), s32[]{:S(2)}) async-start(), calls=%async_computation.1 | async-start | bytes 524288 | tf_op jit(solution)/shard_map/psum | solution.py:14
  57.9 80.2 %copy-start.1 = (f32[32,2048]{1,0:T(8,128)S(1)}, f32[32,2048]{1,0:T(8,128)}, u32[]{:S(2)}) copy-start(f32[32,2048]{1,0:T(8,128)} %all-reduce.11.cloned.1.call-done) | copy-start | bytes 786436
  58.0 74.1 %all-reduce.15.cloned.1.call-start = ((), (), s32[]{:S(2)}) async-start(), calls=%async_computation.2 | async-start | bytes 524288 | tf_op jit(solution)/shard_map/psum | solution.py:21
  100.2 80.1 %all-reduce.17.cloned.1.call-start = ((), (), s32[]{:S(2)}) async-start(), calls=%async_computation.3 | async-start | bytes 524288 | tf_op jit(solution)/shard_map/psum | solution.py:14
  144.9 74.1 %all-reduce.19.cloned.1.call-start = ((), (), s32[]{:S(2)}) async-start(), calls=%async_computation.4 | async-start | bytes 524288 | tf_op jit(solution)/shard_map/psum | solution.py:21
  187.2 110.7 %copy-start.2 = (f32[32,2048]{1,0:T(8,128)S(1)}, f32[32,2048]{1,0:T(8,128)}, u32[]{:S(2)}) copy-start(f32[32,2048]{1,0:T(8,128)} %all-reduce.15.cloned.1.call-done) | copy-start | bytes 786436
  187.2 73.1 %all-reduce.21.cloned.1.call-start = ((), (), s32[]{:S(2)}) async-start(), calls=%async_computation.5 | async-start | bytes 524288 | tf_op jit(solution)/shard_map/psum | solution.py:32
  224.8 73.1 %all-reduce.23.cloned.1.call-start = ((), (), s32[]{:S(2)}) async-start(), calls=%async_computation.6 | async-start | bytes 524288 | tf_op jit(solution)/shard_map/psum | solution.py:25
  266.0 78.1 %copy-start.3 = (f32[32,2048]{1,0:T(8,128)S(1)}, f32[32,2048]{1,0:T(8,128)}, u32[]{:S(2)}) copy-start(f32[32,2048]{1,0:T(8,128)} %all-reduce.21.cloned.1.call-done) | copy-start | bytes 786436
  266.0 73.1 %all-reduce.25.cloned.1.call-start = ((), (), s32[]{:S(2)}) async-start(), calls=%async_computation.7 | async-start | bytes 524288 | tf_op jit(solution)/shard_map/psum | solution.py:32
  303.6 78.1 %all-reduce.27.cloned.1.call-start = ((), (), s32[]{:S(2)}) async-start(), calls=%async_computation.8 | async-start | bytes 524288 | tf_op jit(solution)/shard_map/psum | solution.py:25
  344.2 43.3 %copy-start.4 = (f32[32,2048]{1,0:T(8,128)S(1)}, f32[32,2048]{1,0:T(8,128)}, u32[]{:S(2)}) copy-start(f32[32,2048]{1,0:T(8,128)} %all-reduce.19.cloned.1.call-done) | copy-start | bytes 786436
  344.2 78.8 %copy-start.5 = (f32[32,2048]{1,0:T(8,128)S(1)}, f32[32,2048]{1,0:T(8,128)}, u32[]{:S(2)}) copy-start(f32[32,2048]{1,0:T(8,128)} %all-reduce.25.cloned.1.call-done) | copy-start | bytes 786436
  349.9 73.1 %all-reduce.29.cloned.1.call-start = ((), (), s32[]{:S(2)}) async-start(), calls=%async_computation.9 | async-start | bytes 524288 | tf_op jit(solution)/shard_map/psum | solution.py:32
Sparse Core Ops, SparseCore 0:
  16.4 34.6 all-reduce.10
  58.1 35.3 all-reduce.12
  100.4 31.6 all-reduce.14
  145.0 35.3 all-reduce.16
  187.3 31.6 all-reduce.18
  224.9 35.3 all-reduce.20
  266.1 31.6 all-reduce.22
  303.8 35.3 all-reduce.24
  350.0 31.6 all-reduce.26
  387.6 35.2 all-reduce.28
where the time goes:
time: 432 us
  waiting for transfers between devices  338 us (78%)
  matrix products  74.4 us (17%)
  between operations  14.2 us (3%)
    psum x3, waiting for transfers between devices, backward_diag(): return lax.psum(partial_value, 'rows')  105 us
    psum x3, waiting for transfers between devices, forward_diag(): return lax.psum(partial_value, 'cols')  98.4 us
    psum x2, waiting for transfers between devices, forward_couple(): return lax.psum(partial_value, 'rows')  70.7 us
    psum x2, waiting for transfers between devices, backward_couple(): return lax.psum(partial_value, 'cols')  63.6 us
    dot_general x3, matrix products, forward_diag(): jnp.einsum('lm,im->li', resid.astype(jnp.bfloat16), tile, preferred_eleme...  20.2 us
    dot_general x3, matrix products, lower_term(): jnp.einsum('lj,ij->li', vector_bf, block, preferred_element_type=jnp.floa...  19.5 us
    dot_general x3, matrix products, backward_diag(): jnp.einsum('li,im->lm', resid.astype(jnp.bfloat16), tile, preferred_eleme...  17.2 us
    dot_general x3, matrix products, upper_term(): jnp.einsum('li,ij->lj', vector_bf, block, preferred_element_type=jnp.floa...  16.4 us
  transfers between devices with their start and end apart: 10, of which 10 were waited for; matrix products, arithmetic and copies ran while one was open for 0% of the time, Pallas kernels for 0%

commit v1 on v0

--- a/solution.py
+++ b/solution.py
@@ -18,7 +18,7 @@
     partial_value = jnp.einsum(
         "lm,im->li", resid.astype(jnp.bfloat16), tile, preferred_element_type=jnp.float32
     )
-    return lax.psum(partial_value, "cols")
+    return jnp.sum(lax.all_gather(partial_value, "cols"), axis=0)
 
 
 def backward_couple(partial_value):

time: 432 us -> 390 us (0.903)
  waiting for transfers between devices: 338 us -> 292 us
    psum x3 -> x0, waiting for transfers between devices: 98.4 us -> none  [forward_diag(): return lax.psum(partial_value, 'cols')]
    all_gather x0 -> x3, waiting for transfers between devices: none -> 52.6 us  [forward_diag(): return jnp.sum(lax.all_gather(partial_value, 'cols'), axis=0)]
where the time goes in v1:
time: 390 us
  waiting for transfers between devices  292 us (75%)
  matrix products  74.1 us (19%)
  between operations  14.2 us (4%)
  other arithmetic  6.73 us (2%)
    psum x3, waiting for transfers between devices, backward_diag(): return lax.psum(partial_value, 'rows')  105 us
    psum x2, waiting for transfers between devices, forward_couple(): return lax.psum(partial_value, 'rows')  70.7 us
    psum x2, waiting for transfers between devices, backward_couple(): return lax.psum(partial_value, 'cols')  63.6 us
    all_gather x3, waiting for transfers between devices, forward_diag(): return jnp.sum(lax.all_gather(partial_value, 'cols'), axis=0)  52.6 us
    dot_general x3, matrix products, forward_diag(): jnp.einsum('lm,im->li', resid.astype(jnp.bfloat16), tile, preferred_eleme...  20.2 us
    dot_general x3, matrix products, lower_term(): jnp.einsum('lj,ij->li', vector_bf, block, preferred_element_type=jnp.floa...  19.3 us
    dot_general x3, matrix products, backward_diag(): jnp.einsum('li,im->lm', resid.astype(jnp.bfloat16), tile, preferred_eleme...  17.1 us
    dot_general x3, matrix products, upper_term(): jnp.einsum('li,ij->lj', vector_bf, block, preferred_element_type=jnp.floa...  16.4 us
  transfers between devices with their start and end apart: 10, of which 10 were waited for; matrix products, arithmetic and copies ran while one was open for 0% of the time, Pallas kernels for 0%

profile of v1, /device:TPU:0, one launch (start us, length us, event | category | flops | bytes accessed | tf_op | source)
XLA Modules:
  0.0 389.6 jit_solution(5442025086355451501)
XLA Ops:
  7.2 0.0 all-gather.7.cloned.1.call-start
  7.2 1.4 copy-done
  8.6 1.0 convolution_bitcast_fusion
  9.6 6.7 %fusion.22 = f32[32,2048]{1,0:T(8,128)} fusion(bf16[3,2048,2048]{2,1,0:T(8,128)(2,1)} %param.5, f32[3,32,2048]{2,1,0:T(8,128)S(1)} %convolution_bitcast_fusion), kind=kOutput, calls=%fused_computation.22 | convolution fusion | flops 268435456 | bytes 8781824 | tf_op jit(solution)/shard_map/lm,im->li/dot_general | solution.py:18
  16.3 0.0 all-gather.7.cloned.1.call-update
  16.3 0.0 all-reduce.8.cloned.1.call-start
  16.4 19.5 %all-gather.7.cloned.1.call-done = f32[128,2048]{1,0:T(8,128)} async-done(((f32[32,2048]{1,0:T(8,128)}), f32[128,2048]{1,0:T(8,128)}) %all-gather.7.cloned.1.call-update) | async-done | bytes 1048592 | tf_op jit(solution)/shard_map/all_gather | solution.py:21
  35.9 1.3 reduce_sum.27
  37.2 6.7 %fusion.14 = f32[32,2048]{1,0:T(8,128)} fusion(bf16[3,2048,2048]{2,1,0:T(8,128)(2,1)} %param.4, f32[32,2048]{1,0:T(8,128)S(1)} %reduce_sum.27), kind=kOutput, calls=%fused_computation.14 | convolution fusion | flops 268500992 | bytes 8912896 | tf_op jit(solution)/shard_map/lj,ij->li/dot_general | solution.py:36
  43.9 0.0 all-reduce.8.cloned.1.call-update
  43.9 0.0 all-gather.9.cloned.1.call-start
  44.0 35.5 %all-reduce.8.cloned.1.call-done = f32[32,2048]{1,0:T(8,128)} async-done(((f32[32,2048]{1,0:T(8,128)}), f32[32,2048]{1,0:T(8,128)}) %all-reduce.8.cloned.1.call-update) | async-done | bytes 262160 | tf_op jit(solution)/shard_map/psum | solution.py:14
  79.4 6.8 %fusion.10 = f32[32,2048]{1,0:T(8,128)} fusion(bf16[3,2048,2048]{2,1,0:T(8,128)(2,1)} %param.5, f32[32,2048]{1,0:T(8,128)} %all-reduce.8.cloned.1.call-done, f32[3,32,2048]{2,1,0:T(8,128)S(1)} %convolution_bitcast_fusion), kind=kOutput, calls=%fused_computation.10 | convolution fusion | flops 268566528 | bytes 9175040 | tf_op jit(solution)/shard_map/lm,im->li/dot_general | solution.py:18
  86.2 0.0 all-gather.9.cloned.1.call-update
  86.2 0.0 all-reduce.10.cloned.1.call-start
  86.3 16.6 %all-gather.9.cloned.1.call-done = f32[128,2048]{1,0:T(8,128)} async-done(((f32[32,2048]{1,0:T(8,128)}), f32[128,2048]{1,0:T(8,128)}) %all-gather.9.cloned.1.call-update) | async-done | bytes 1048592 | tf_op jit(solution)/shard_map/all_gather | solution.py:21
  102.8 1.3 reduce_sum.28
  104.1 6.0 %fusion.6 = f32[32,2048]{1,0:T(8,128)S(1)} fusion(bf16[3,2048,2048]{2,1,0:T(8,128)(2,1)} %param.4, f32[32,2048]{1,0:T(8,128)S(1)} %reduce_sum.28), kind=kOutput, calls=%fused_computation.6 | convolution fusion | flops 268500992 | bytes 8912896 | tf_op jit(solution)/shard_map/lj,ij->li/dot_general | solution.py:36
  110.1 6.7 %fusion.39 = f32[32,2048]{1,0:T(8,128)} fusion(f32[32,2048]{1,0:T(8,128)S(1)} %fusion.6, bf16[3,2048,2048]{2,1,0:T(8,128)(2,1)} %param.4, f32[32,2048]{1,0:T(8,128)S(1)} %reduce_sum.27), kind=kOutput, calls=%fused_computation.38 | convolution fusion | flops 268566528 | bytes 9175040 | tf_op jit(solution)/shard_map/lj,ij->li/dot_general | solution.py:36
  116.8 0.0 all-reduce.10.cloned.1.call-update
  116.8 0.2 all-gather.11.cloned.1.call-start
  117.1 35.2 %all-reduce.10.cloned.1.call-done = f32[32,2048]{1,0:T(8,128)} async-done(((f32[32,2048]{1,0:T(8,128)}), f32[32,2048]{1,0:T(8,128)}) %all-reduce.10.cloned.1.call-update) | async-done | bytes 262160 | tf_op jit(solution)/shard_map/psum | solution.py:14
  152.3 6.8 %fusion.2 = f32[32,2048]{1,0:T(8,128)} fusion(bf16[3,2048,2048]{2,1,0:T(8,128)(2,1)} %param.5, f32[32,2048]{1,0:T(8,128)} %all-reduce.10.cloned.1.call-done, f32[3,32,2048]{2,1,0:T(8,128)S(1)} %convolution_bitcast_fusion), kind=kOutput, calls=%fused_computation.2 | convolution fusion | flops 268566528 | bytes 9175040 | tf_op jit(solution)/shard_map/lm,im->li/dot_general | solution.py:18
  159.1 0.0 all-reduce.12.cloned.1.call-start
  159.1 16.6 %all-gather.11.cloned.1.call-done = f32[128,2048]{1,0:T(8,128)} async-done(((f32[32,2048]{1,0:T(8,128)}), f32[128,2048]{1,0:T(8,128)}) %all-gather.11.cloned.1.call-update) | async-done | bytes 1048592 | tf_op jit(solution)/shard_map/all_gather | solution.py:21
  175.7 1.3 reduce_sum.29
  177.0 5.6 %fusion = f32[32,2048]{1,0:T(8,128)} fusion(bf16[3,2048,2048]{2,1,0:T(8,128)(2,1)} %param.5, f32[32,2048]{1,0:T(8,128)S(1)} %reduce_sum.29), kind=kOutput, calls=%fused_computation | convolution fusion | flops 268500992 | bytes 8912896 | tf_op jit(solution)/shard_map/li,im->lm/dot_general | solution.py:29
  182.6 0.0 all-reduce.12.cloned.1.call-update
  182.7 0.0 all-reduce.14.cloned.1.call-start
  182.7 35.5 %all-reduce.12.cloned.1.call-done = f32[32,2048]{1,0:T(8,128)} async-done(((f32[32,2048]{1,0:T(8,128)}), f32[32,2048]{1,0:T(8,128)}) %all-reduce.12.cloned.1.call-update) | async-done | bytes 262160 | tf_op jit(solution)/shard_map/psum | solution.py:32
  218.2 5.7 %fusion.4 = f32[32,2048]{1,0:T(8,128)} fusion(bf16[3,2048,2048]{2,1,0:T(8,128)(2,1)} %param.4, f32[32,2048]{1,0:T(8,128)} %all-reduce.12.cloned.1.call-done), kind=kOutput, calls=%fused_computation.4 | convolution fusion | flops 268500992 | bytes 8912896 | tf_op jit(solution)/shard_map/li,ij->lj/dot_general | solution.py:40
  223.9 0.0 all-reduce.14.cloned.1.call-update
  223.9 0.0 all-reduce.16.cloned.1.call-start
  224.0 31.8 %all-reduce.14.cloned.1.call-done = f32[32,2048]{1,0:T(8,128)} async-done(((f32[32,2048]{1,0:T(8,128)}), f32[32,2048]{1,0:T(8,128)}) %all-reduce.14.cloned.1.call-update) | async-done | bytes 262160 | tf_op jit(solution)/shard_map/psum | solution.py:25
  255.8 5.7 %fusion.8 = f32[32,2048]{1,0:T(8,128)} fusion(bf16[3,2048,2048]{2,1,0:T(8,128)(2,1)} %param.5, f32[32,2048]{1,0:T(8,128)S(1)} %reduce_sum.28, f32[32,2048]{1,0:T(8,128)} %all-reduce.14.cloned.1.call-done), kind=kOutput, calls=%fused_computation.8 | convolution fusion | flops 268566528 | bytes 9175040 | tf_op jit(solution)/shard_map/li,im->lm/dot_general | solution.py:29
  261.5 0.0 all-reduce.16.cloned.1.call-update
  261.5 0.0 all-reduce.18.cloned.1.call-start
  261.6 35.4 %all-reduce.16.cloned.1.call-done = f32[32,2048]{1,0:T(8,128)} async-done(((f32[32,2048]{1,0:T(8,128)}), f32[32,2048]{1,0:T(8,128)}) %all-reduce.16.cloned.1.call-update) | async-done | bytes 262160 | tf_op jit(solution)/shard_map/psum | solution.py:32
  297.0 5.0 %fusion.12 = f32[32,2048]{1,0:T(8,128)S(1)} fusion(bf16[3,2048,2048]{2,1,0:T(8,128)(2,1)} %param.4, f32[32,2048]{1,0:T(8,128)} %all-reduce.16.cloned.1.call-done), kind=kOutput, calls=%fused_computation.12 | convolution fusion | flops 268500992 | bytes 8912896 | tf_op jit(solution)/shard_map/li,ij->lj/dot_general | solution.py:40
  302.0 5.7 %fusion.42 = f32[32,2048]{1,0:T(8,128)} fusion(f32[32,2048]{1,0:T(8,128)S(1)} %fusion.12, bf16[3,2048,2048]{2,1,0:T(8,128)(2,1)} %param.4, f32[32,2048]{1,0:T(8,128)S(1)} %copy-done.1), kind=kOutput, calls=%fused_computation.39 | convolution fusion | flops 268566528 | bytes 9175040 | tf_op jit(solution)/shard_map/li,ij->lj/dot_general | solution.py:40
  307.7 0.0 all-reduce.18.cloned.1.call-update
  307.8 0.0 all-reduce.20.cloned.1.call-start
  307.8 31.8 %all-reduce.18.cloned.1.call-done = f32[32,2048]{1,0:T(8,128)} async-done(((f32[32,2048]{1,0:T(8,128)}), f32[32,2048]{1,0:T(8,128)}) %all-reduce.18.cloned.1.call-update) | async-done | bytes 262160 | tf_op jit(solution)/shard_map/psum | solution.py:25
  339.6 5.7 %fusion.36 = f32[1,32,2048]{2,1,0:T(8,128)} fusion(bf16[3,2048,2048]{2,1,0:T(8,128)(2,1)} %param.5, f32[32,2048]{1,0:T(8,128)S(1)} %reduce_sum.27, f32[32,2048]{1,0:T(8,128)} %all-reduce.18.cloned.1.call-done), kind=kOutput, calls=%fused_computation.37 | convolution fusion | flops 268566528 | bytes 9175040 | tf_op jit(solution)/shard_map/li,im->lm/dot_general | solution.py:29
  345.3 0.0 all-reduce.20.cloned.1.call-update
  345.4 0.9 pad_maximum_fusion.1
  346.3 34.5 %all-reduce.20.cloned.1.call-done = f32[1,32,2048]{2,1,0:T(8,128)} async-done(((f32[1,32,2048]{2,1,0:T(8,128)}), f32[1,32,2048]{2,1,0:T(8,128)}) %all-reduce.20.cloned.1.call-update) | async-done | bytes 262160 | tf_op jit(solution)/shard_map/psum | solution.py:32
  380.8 1.9 pad_maximum_fusion
  (6 shorter events, 0.0 us)
Async XLA Ops:
  7.2 1.4 copy-start
  7.2 28.7 %all-gather.7.cloned.1.call-start = ((), (), s32[]{:S(2)}) async-start(), calls=%async_computation.7 | async-start | bytes 1310720 | tf_op jit(solution)/shard_map/all_gather | solution.py:21
  16.3 63.1 %all-reduce.8.cloned.1.call-start = ((), (), s32[]{:S(2)}) async-start(), calls=%async_computation | async-start | bytes 524288 | tf_op jit(solution)/shard_map/psum | solution.py:14
  43.9 58.9 %all-gather.9.cloned.1.call-start = ((), (), s32[]{:S(2)}) async-start(), calls=%async_computation.8 | async-start | bytes 1310720 | tf_op jit(solution)/shard_map/all_gather | solution.py:21
  86.2 66.1 %all-reduce.10.cloned.1.call-start = ((), (), s32[]{:S(2)}) async-start(), calls=%async_computation.1 | async-start | bytes 524288 | tf_op jit(solution)/shard_map/psum | solution.py:14
  116.8 58.9 %all-gather.11.cloned.1.call-start = ((), (), s32[]{:S(2)}) async-start(), calls=%async_computation.9 | async-start | bytes 1310720 | tf_op jit(solution)/shard_map/all_gather | solution.py:21
  159.1 59.1 %all-reduce.12.cloned.1.call-start = ((), (), s32[]{:S(2)}) async-start(), calls=%async_computation.2 | async-start | bytes 524288 | tf_op jit(solution)/shard_map/psum | solution.py:32
  182.7 73.1 %all-reduce.14.cloned.1.call-start = ((), (), s32[]{:S(2)}) async-start(), calls=%async_computation.3 | async-start | bytes 524288 | tf_op jit(solution)/shard_map/psum | solution.py:25
  223.9 78.1 %copy-start.1 = (f32[32,2048]{1,0:T(8,128)S(1)}, f32[32,2048]{1,0:T(8,128)}, u32[]{:S(2)}) copy-start(f32[32,2048]{1,0:T(8,128)} %all-reduce.12.cloned.1.call-done) | copy-start | bytes 786436
  223.9 73.1 %all-reduce.16.cloned.1.call-start = ((), (), s32[]{:S(2)}) async-start(), calls=%async_computation.4 | async-start | bytes 524288 | tf_op jit(solution)/shard_map/psum | solution.py:32
  261.5 78.1 %all-reduce.18.cloned.1.call-start = ((), (), s32[]{:S(2)}) async-start(), calls=%async_computation.5 | async-start | bytes 524288 | tf_op jit(solution)/shard_map/psum | solution.py:25
  302.0 78.8 %copy-start.2 = (f32[32,2048]{1,0:T(8,128)S(1)}, f32[32,2048]{1,0:T(8,128)}, u32[]{:S(2)}) copy-start(f32[32,2048]{1,0:T(8,128)} %all-reduce.16.cloned.1.call-done) | copy-start | bytes 786436
  307.8 73.1 %all-reduce.20.cloned.1.call-start = ((), (), s32[]{:S(2)}) async-start(), calls=%async_computation.6 | async-start | bytes 524288 | tf_op jit(solution)/shard_map/psum | solution.py:32
Sparse Core Ops, SparseCore 0:
  16.4 19.4 all-gather.6
  44.0 35.3 all-reduce.7
  86.3 16.4 all-gather.8
  117.0 35.2 all-reduce.9
  159.2 16.4 all-gather.10
  182.8 35.3 all-reduce.11
  224.1 31.6 all-reduce.13
  261.7 35.3 all-reduce.15
  307.9 31.6 all-reduce.17
  345.5 35.3 all-reduce.19
